TPU v7x, 32 devices: a whole 2x2x4 slice. The times are simulated.
32 devices in a mesh: group: 2 (over y), tm: 4 (over z), mp: 4 (over x, core).
Axes of the slice: x: 2, y: 2, z: 4, core: 2. Of those that a mesh axis runs over, the one named last changes fastest.
Arguments:
- latents: bfloat16 [2, 4, 256, 1536], P('group', 'tm'), parts along dimension 0, may hold values from -6 to 6
- gsd_table: float32 [8, 6, 1536], replicated, may hold values from -3 to 3
- gsd_bucket: int32 [2, 4], P('group', 'tm'), parts along dimension 0, may hold values from 0 to 7
- clearest: int32 [2], P('group'), parts along dimension 0, may hold values from 0 to 3, as said below
- clouds: int32 [2, 4, 256], P('group'), parts along dimension 0, may hold values from 0 to 1
- cross_query: bfloat16 [1536, 1536], P('tm', 'mp'), may hold values from -5 to 5
- cross_pairs: bfloat16 [1536, 2, 1536], P('tm', None, 'mp'), may hold values from -5 to 5
- cross_merge: bfloat16 [1536, 1536], P('mp', 'tm'), may hold values from -0.15625 to 0.15625
- time_triple: bfloat16 [1536, 3, 1536], P('tm', None, 'mp'), may hold values from -5 to 5
- time_merge: bfloat16 [1536, 1536], P('mp', 'tm'), may hold values from -0.15625 to 0.15625
Outputs:
- updated: bfloat16 [2, 4, 256, 1536], P('group', 'tm'), parts along dimension 0
There are 2 independent parts, one for each index of `group`. A program takes and returns all parts, laid end to end along the dimension named above; an argument that names none is the same for every part. Nothing has to cross between parts.
Inputs may be any that keep to these rules, and one draw needn't show every extreme that they name: clearest[s] is one of the stack's dates; that date has no cloudy token, and no date of stack s has fewer cloudy tokens.
All inputs are finite; a program needn't handle non-finite values.
Results may differ from a plain program's by a relative error of at most 0.014.
The roundings to bfloat16 on the way count: a program that leaves them out, or rounds other values in their place, can miss the bound.
Values may be sent and summed in bfloat16 or wider, within the bound.
A program may use at most 64 MiB of HBM per device.

v0:
```python
import jax
import jax.numpy as jnp
from jax import lax
from jax.sharding import PartitionSpec as P

HEAD_DIM = 64


def broadcast(block, axis, holder):
    block = jnp.where(lax.axis_index(axis) == holder, block, jnp.zeros_like(block))
    return lax.psum(block, axis)


def normalize(values):
    centre = jnp.mean(values, axis=-1, keepdims=True)
    shifted = values - centre
    variance = jnp.mean(shifted * shifted, axis=-1, keepdims=True)
    return shifted * lax.rsqrt(variance + 1e-06)


def softmax_rows(scores):
    highest = jnp.max(scores, axis=-1, keepdims=True)
    weights = jnp.exp(scores - highest)
    return weights / jnp.sum(weights, axis=-1, keepdims=True)


def shards(
    latents,
    gsd_table,
    gsd_bucket,
    clearest,
    clouds,
    cross_query,
    cross_pairs,
    cross_merge,
    time_triple,
    time_merge,
):
    stacks = latents.shape[0]
    seq_tokens = latents.shape[2]
    model_width = latents.shape[3]
    local_width = cross_query.shape[1]
    local_heads = local_width // HEAD_DIM
    buckets = gsd_table.shape[0]
    scale_factor = HEAD_DIM ** (-0.5)
    my_buckets = gsd_bucket.reshape(stacks)
    one_hot = (my_buckets[:, None] == jnp.arange(buckets, dtype=jnp.int32)[None, :]).astype(
        jnp.float32
    )
    modulation = jnp.dot(
        one_hot, gsd_table.reshape(buckets, 6 * model_width), precision=lax.Precision.HIGHEST
    ).reshape(stacks, 6, 1, 1, model_width)
    values = latents.astype(jnp.float32)
    normed = (normalize(values) * (1.0 + modulation[:, 1]) + modulation[:, 0]).astype(jnp.bfloat16)
    full_query, full_pairs, full_merge, full_triple, full_time = (
        lax.all_gather(cross_query, "tm", axis=0, tiled=True),
        lax.all_gather(cross_pairs, "tm", axis=0, tiled=True),
        lax.all_gather(cross_merge, "tm", axis=1, tiled=True),
        lax.all_gather(time_triple, "tm", axis=0, tiled=True),
        lax.all_gather(time_merge, "tm", axis=1, tiled=True),
    )
    flat_rows = normed.reshape(stacks * seq_tokens, model_width)
    queries = jnp.dot(flat_rows, full_query, preferred_element_type=jnp.float32).astype(
        jnp.bfloat16
    )

    def project_reference(ref_rows):
        return jnp.einsum(
            "ld,dce->lce", ref_rows, full_pairs, preferred_element_type=jnp.float32
        ).astype(jnp.bfloat16)

    def empty_pairs(ref_rows):
        return jnp.zeros((ref_rows.shape[0], 2, local_width), jnp.bfloat16)

    position = lax.axis_index("tm")
    owner_date = clearest[0]
    local_pair = lax.cond(position == owner_date, project_reference, empty_pairs, normed[0, 0])
    key_pair = broadcast(local_pair, "tm", owner_date)
    pair_list = [key_pair]
    key_pairs = jnp.stack(pair_list)
    heads_query = queries.reshape(stacks, seq_tokens, local_heads, HEAD_DIM)
    heads_key = key_pairs[:, :, 0].reshape(stacks, seq_tokens, local_heads, HEAD_DIM)
    heads_value = key_pairs[:, :, 1].reshape(stacks, seq_tokens, local_heads, HEAD_DIM)
    scores = (
        jnp.einsum("sqhe,skhe->shqk", heads_query, heads_key, preferred_element_type=jnp.float32)
        * scale_factor
    )
    attn_weights = softmax_rows(scores).astype(jnp.bfloat16)
    attended = jnp.einsum(
        "shqk,skhe->sqhe", attn_weights, heads_value, preferred_element_type=jnp.float32
    ).astype(jnp.bfloat16)
    cross_terms = jnp.dot(
        attended.reshape(stacks * seq_tokens, local_width),
        full_merge,
        preferred_element_type=jnp.float32,
    )
    cross_sum = lax.psum(cross_terms.astype(jnp.bfloat16), "mp").astype(jnp.float32)
    middle = values + modulation[:, 2] * cross_sum.reshape(stacks, 1, seq_tokens, model_width)
    normed_two = (normalize(middle) * (1.0 + modulation[:, 4]) + modulation[:, 3]).astype(
        jnp.bfloat16
    )
    triple = jnp.einsum(
        "nd,dce->nce",
        normed_two.reshape(stacks * seq_tokens, model_width),
        full_triple,
        preferred_element_type=jnp.float32,
    ).astype(jnp.bfloat16)
    triple = triple.reshape(stacks, 1, seq_tokens, 3, local_width)
    patches = lax.all_to_all(triple, "tm", split_axis=2, concat_axis=1, tiled=True)
    date_count = patches.shape[1]
    patch_count = patches.shape[2]
    allowed = lax.dynamic_slice_in_dim(clouds == 0, position * patch_count, patch_count, 2)
    split_heads = patches.reshape(stacks, date_count, patch_count, 3, local_heads, HEAD_DIM)
    scores_time = (
        jnp.einsum(
            "sdphe,sfphe->sphdf",
            split_heads[:, :, :, 0],
            split_heads[:, :, :, 1],
            preferred_element_type=jnp.float32,
        )
        * scale_factor
    )
    visible = jnp.transpose(allowed, (0, 2, 1))[:, :, None, None, :]
    scores_time = jnp.where(visible, scores_time, -1e30)
    time_weights = softmax_rows(scores_time).astype(jnp.bfloat16)
    mixed_out = jnp.einsum(
        "sphdf,sfphe->sdphe",
        time_weights,
        split_heads[:, :, :, 2],
        preferred_element_type=jnp.float32,
    ).astype(jnp.bfloat16)
    mixed_out = mixed_out.reshape(stacks, date_count, patch_count, local_width)
    returned = lax.all_to_all(mixed_out, "tm", split_axis=1, concat_axis=2, tiled=True)
    time_terms = jnp.dot(
        returned.reshape(stacks * seq_tokens, local_width),
        full_time,
        preferred_element_type=jnp.float32,
    )
    time_sum = lax.psum(time_terms.astype(jnp.bfloat16), "mp").astype(jnp.float32)
    return (
        middle + modulation[:, 5] * time_sum.reshape(stacks, 1, seq_tokens, model_width)
    ).astype(jnp.bfloat16)


def solution(mesh):
    placed = (
        P("group", "tm", None, None),
        P(),
        P("group", "tm"),
        P("group"),
        P("group", None, None),
        P("tm", "mp"),
        P("tm", None, "mp"),
        P("mp", "tm"),
        P("tm", None, "mp"),
        P("mp", "tm"),
    )
    return jax.shard_map(
        shards, mesh=mesh, in_specs=placed, out_specs=P("group", "tm", None, None), check_vma=False
    )
```

profile of v0, /device:TPU:0, one launch (start us, length us, event | category | flops | bytes accessed | tf_op | source)
XLA Modules:
  0.0 375.0 jit_solution(14642475833497510122)
XLA Ops:
  6.5 2.0 copy.47
  12.1 50.1 %all-gather.6.cloned.1.call-done = bf16[1536,2,384]{2,0,1:T(8,128)(2,1)} async-done(((bf16[384,2,384]{2,0,1:T(8,128)(2,1)}), bf16[1536,2,384]{2,0,1:T(8,128)(2,1)}) %all-gather.6.cloned.1.call-update) | async-done | bytes 2359312 | tf_op jit(solution)/shard_map/all_gather | solution.py:57
  62.2 0.8 select_bitcast_fusion
  63.7 29.4 %all-gather.8.cloned.1.call-done = bf16[1536,384]{1,0:T(8,128)(2,1)} async-done(((bf16[384,384]{1,0:T(8,128)(2,1)}), bf16[1536,384]{1,0:T(8,128)(2,1)}) %all-gather.8.cloned.1.call-update) | async-done | bytes 1179664 | tf_op jit(solution)/shard_map/all_gather | solution.py:56
  93.0 1.8 convolution_convert_fusion.5
  95.0 36.6 %all-reduce.4.cloned.1.call-done = bf16[1,256,2,384]{3,1,2,0:T(8,128)(2,1)} async-done(((bf16[1,256,2,384]{3,1,2,0:T(8,128)(2,1)}), bf16[1,256,2,384]{3,1,2,0:T(8,128)(2,1)}) %all-reduce.4.cloned.1.call-update) | async-done | bytes 393232 | tf_op jit(solution)/shard_map/psum | solution.py:11
  131.6 1.1 fusion.44
  133.9 29.0 %all-gather.10.cloned.1.call-done = bf16[384,1536]{1,0:T(8,128)(2,1)} async-done(((bf16[384,384]{1,0:T(8,128)(2,1)}), bf16[384,1536]{1,0:T(8,128)(2,1)}) %all-gather.10.cloned.1.call-update) | async-done | bytes 1179664 | tf_op jit(solution)/shard_map/all_gather | solution.py:58
  162.9 2.7 convolution_convert_fusion.2
  166.2 33.6 %all-reduce.6.cloned.1.call-done = bf16[256,1536]{1,0:T(8,128)(2,1)} async-done(((bf16[256,1536]{1,0:T(8,128)(2,1)}), bf16[256,1536]{1,0:T(8,128)(2,1)}) %all-reduce.6.cloned.1.call-update) | async-done | bytes 786448 | tf_op jit(solution)/shard_map/psum | solution.py:97
  199.9 1.5 fusion.16
  201.9 69.5 %all-gather.12.cloned.1.call-done = bf16[1536,3,384]{2,0,1:T(8,128)(2,1)} async-done(((bf16[384,3,384]{2,0,1:T(8,128)(2,1)}), bf16[1536,3,384]{2,0,1:T(8,128)(2,1)}) %all-gather.12.cloned.1.call-update) | async-done | bytes 3538960 | tf_op jit(solution)/shard_map/all_gather | solution.py:59
  271.4 3.2 fusion.12
  274.7 1.4 copy.52
  276.1 4.2 %all-to-all-start = ((bf16[1,1,256,3,384]{4,3,1,0,2:T(4,128)(2,1)}), bf16[1,1,256,3,384]{4,3,1,0,2:T(4,128)(2,1)}, u32[]{:S(2)}, u32[]{:S(2)}) async-start(bf16[1,1,256,3,384]{4,3,1,0,2:T(4,128)(2,1)} %copy.52), calls=%async_computation | async-start | bytes 1572864 | tf_op jit(solution)/shard_map/all_to_all | solution.py:109
  281.1 31.1 %all-to-all-done = bf16[1,1,256,3,384]{4,3,1,0,2:T(4,128)(2,1)} async-done(((bf16[1,1,256,3,384]{4,3,1,0,2:T(4,128)(2,1)}), bf16[1,1,256,3,384]{4,3,1,0,2:T(4,128)(2,1)}, u32[]{:S(2)}, u32[]{:S(2)}) %all-to-all-start) | async-done | bytes 589856 | tf_op jit(solution)/shard_map/all_to_all | solution.py:109
  312.2 2.7 reshape.227
  315.0 1.1 fusion.43
  318.1 1.0 reshape.221
  319.1 3.4 all-to-all-start.1
  322.5 6.1 %all-to-all-done.1 = bf16[1,4,64,384]{3,2,0,1:T(8,128)(2,1)S(1)} async-done(((bf16[1,4,64,384]{3,2,0,1:T(8,128)(2,1)}), bf16[1,4,64,384]{3,2,0,1:T(8,128)(2,1)S(1)}, u32[]{:S(2)}, u32[]{:S(2)}) %all-to-all-start.1) | async-done | bytes 196640 | tf_op jit(solution)/shard_map/all_to_all | solution.py:133
  328.7 2.7 convolution_convert_fusion.1
  331.4 34.3 %all-reduce.8.cloned.1.call-done = bf16[256,1536]{1,0:T(8,128)(2,1)} async-done(((bf16[256,1536]{1,0:T(8,128)(2,1)}), bf16[256,1536]{1,0:T(8,128)(2,1)}) %all-reduce.8.cloned.1.call-update) | async-done | bytes 786448 | tf_op jit(solution)/shard_map/psum | solution.py:139
  365.8 2.4 fusion.10
  (53 shorter events, 8.2 us)
Async XLA Ops:
  6.5 3.5 copy-start
  6.5 4.6 %copy-start.1 = (bf16[1,1,256,1536]{3,2,1,0:T(8,128)(2,1)S(1)}, bf16[1,1,256,1536]{3,2,1,0:T(8,128)(2,1)}, u32[]{:S(2)}) copy-start(bf16[1,1,256,1536]{3,2,1,0:T(8,128)(2,1)} %param.12) | copy-start | bytes 2359300
  6.5 55.6 %all-gather.6.cloned.1.call-start = ((), (), s32[]{:S(2)}) async-start(), calls=%async_computation.2 | async-start | bytes 2949120 | tf_op jit(solution)/shard_map/all_gather | solution.py:57
  8.6 84.4 %all-gather.8.cloned.1.call-start = ((), (), s32[]{:S(2)}) async-start(), calls=%async_computation.4 | async-start | bytes 1474560 | tf_op jit(solution)/shard_map/all_gather | solution.py:56
  9.4 122.2 %all-reduce.4.cloned.1.call-start = ((), (), s32[]{:S(2)}) async-start(), calls=%async_computation.3 | async-start | bytes 786432 | tf_op jit(solution)/shard_map/psum | solution.py:11
  63.0 99.8 %all-gather.10.cloned.1.call-start = ((), (), s32[]{:S(2)}) async-start(), calls=%async_computation.5 | async-start | bytes 1474560 | tf_op jit(solution)/shard_map/all_gather | solution.py:58
  63.6 136.3 %all-reduce.6.cloned.1.call-start = ((), (), s32[]{:S(2)}) async-start(), calls=%async_computation.6 | async-start | bytes 1572864 | tf_op jit(solution)/shard_map/psum | solution.py:97
  165.7 105.8 %all-gather.12.cloned.1.call-start = ((), (), s32[]{:S(2)}) async-start(), calls=%async_computation.7 | async-start | bytes 4423680 | tf_op jit(solution)/shard_map/all_gather | solution.py:59
  199.9 1.6 copy-start.2
  274.7 6.4 %copy-start.4 = (s32[1,4,256]{2,1,0:T(4,128)S(1)}, s32[1,4,256]{2,1,0:T(4,128)}, u32[]{:S(2)}) copy-start(s32[1,4,256]{2,1,0:T(4,128)} %param.16) | copy-start | bytes 12292
  276.1 36.2 %all-to-all-start = ((bf16[1,1,256,3,384]{4,3,1,0,2:T(4,128)(2,1)}), bf16[1,1,256,3,384]{4,3,1,0,2:T(4,128)(2,1)}, u32[]{:S(2)}, u32[]{:S(2)}) async-start(bf16[1,1,256,3,384]{4,3,1,0,2:T(4,128)(2,1)} %copy.52), calls=%async_computation | async-start | bytes 1572864 | tf_op jit(solution)/shard_map/all_to_all | solution.py:109
  280.3 42.3 %all-gather.14.cloned.1.call-start = ((), (), s32[]{:S(2)}) async-start(), calls=%async_computation.8 | async-start | bytes 1474560 | tf_op jit(solution)/shard_map/all_gather | solution.py:60
  316.0 1.4 copy-start.3
  319.1 9.6 %all-to-all-start.1 = ((bf16[1,4,64,384]{3,2,0,1:T(8,128)(2,1)}), bf16[1,4,64,384]{3,2,0,1:T(8,128)(2,1)S(1)}, u32[]{:S(2)}, u32[]{:S(2)}) async-start(bf16[1,4,64,384]{3,2,0,1:T(8,128)(2,1)} %bitcast.30), calls=%async_computation.1 | async-start | bytes 393216 | tf_op jit(solution)/shard_map/all_to_all | solution.py:133
  322.5 43.3 %all-reduce.8.cloned.1.call-start = ((), (), s32[]{:S(2)}) async-start(), calls=%async_computation.9 | async-start | bytes 1572864 | tf_op jit(solution)/shard_map/psum | solution.py:139
Sparse Core Ops, SparseCore 0:
  8.9 53.2 all-gather.5
  63.7 29.2 all-gather.7
  95.4 36.1 all-reduce.3
  133.1 29.7 all-gather.9
  165.8 34.0 all-reduce.5
  201.4 69.9 all-gather.11
  282.8 37.2 all-gather.13
  331.6 34.1 all-reduce.7
where the time goes:
time: 376 us; the launch traced here: 375 us
  waiting for transfers between devices  322 us (86%)
  between operations  15 us (4%)
  matrix products  12.9 us (3%)
  local copies, waits for them, and re-layouts  10.5 us (3%)
  starting transfers between devices  7.84 us (2%)
  other arithmetic  6.42 us (2%)
    all_gather x1, waiting for transfers between devices, shards(): lax.all_gather(time_triple, 'tm', axis=0, tiled=True)  69.5 us
    all_gather x1, waiting for transfers between devices, shards(): lax.all_gather(cross_pairs, 'tm', axis=0, tiled=True)  50.1 us
    psum x1, waiting for transfers between devices, broadcast(): return lax.psum(block, axis)  36.6 us
    psum x1, waiting for transfers between devices, shards(): lax.psum(time_terms.astype(jnp.bfloat16), 'mp').astype(jnp.float32)  34.3 us
    psum x1, waiting for transfers between devices, shards(): lax.psum(cross_terms.astype(jnp.bfloat16), 'mp').astype(jnp.float32)  33.6 us
    all_to_all x1, waiting for transfers between devices, shards(): lax.all_to_all(triple, 'tm', split_axis=2, concat_axis=1, tiled=True)  31.1 us
    all_gather x1, waiting for transfers between devices, shards(): lax.all_gather(cross_query, 'tm', axis=0, tiled=True)  29.4 us
    all_gather x1, waiting for transfers between devices, shards(): lax.all_gather(cross_merge, 'tm', axis=1, tiled=True)  29 us
  transfers between devices with their start and end apart: 10, of which 9 were waited for; matrix products, arithmetic and copies ran while one was open for 4% of the time, Pallas kernels for 0%

commit v1 on v0

--- a/solution.py
+++ b/solution.py
@@ -4,6 +4,27 @@
 from jax.sharding import PartitionSpec as P
 
 HEAD_DIM = 64
+
+
+def hold_scenes(a0, in_dim):
+    frame_out = list(a0.shape[1:])
+    frame_out[in_dim] *= a0.shape[0]
+    return jnp.moveaxis(a0, 0, in_dim).reshape(frame_out)
+
+
+def tell_sources_all_here(sample, axis_tag):
+    taken_in = sample[None]
+    n_slots = lax.axis_size(axis_tag)
+    for to_i in range(n_slots.bit_length() - 1):
+        h_now = 1 << to_i
+        column = []
+        for c in range(n_slots):
+            column.append((c, c ^ h_now))
+        arr_out = lax.ppermute(taken_in, axis_tag, column)
+        before = jnp.stack([taken_in, arr_out])
+        view_out = lax.axis_index(axis_tag) >> to_i & 1
+        taken_in = jnp.where(view_out == 0, before, before[::-1]).reshape(-1, *sample.shape)
+    return taken_in
 
 
 def broadcast(block, axis, holder):
@@ -36,6 +57,10 @@
     time_triple,
     time_merge,
 ):
+
+    def point_run(local_block, own_rows, ndim_at):
+        return hold_scenes(tell_sources_all_here(local_block, own_rows), ndim_at)
+
     stacks = latents.shape[0]
     seq_tokens = latents.shape[2]
     model_width = latents.shape[3]
@@ -56,7 +81,7 @@
         lax.all_gather(cross_query, "tm", axis=0, tiled=True),
         lax.all_gather(cross_pairs, "tm", axis=0, tiled=True),
         lax.all_gather(cross_merge, "tm", axis=1, tiled=True),
-        lax.all_gather(time_triple, "tm", axis=0, tiled=True),
+        point_run(time_triple, "tm", 0),
         lax.all_gather(time_merge, "tm", axis=1, tiled=True),
     )
     flat_rows = normed.reshape(stacks * seq_tokens, model_width)

time: 376 us -> 361 us (0.960)
  waiting for transfers between devices: 322 us -> 282 us
  other arithmetic: 6.42 us -> 18.7 us
  starting transfers between devices: 7.84 us -> 18.1 us
    ppermute x0 -> x2, waiting for transfers between devices: none -> 70.6 us  [tell_sources_all_here(): arr_out = lax.ppermute(taken_in, axis_tag, column)]
    all_gather x1 -> x0, waiting for transfers between devices: 69.5 us -> none  [shards(): lax.all_gather(time_triple, 'tm', axis=0, tiled=True)]
    all_gather x1, waiting for transfers between devices: 50.1 us -> 8.96 us  [shards(): lax.all_gather(cross_pairs, 'tm', axis=0, tiled=True)]
    all_gather x1, waiting for transfers between devices: 29.4 us -> 61.3 us  [shards(): lax.all_gather(cross_query, 'tm', axis=0, tiled=True)]
    psum x1, waiting for transfers between devices: 36.6 us -> 14.1 us  [broadcast(): return lax.psum(block, axis)]
    ppermute x0 -> x2, starting transfers between devices: none -> 9.79 us  [tell_sources_all_here(): arr_out = lax.ppermute(taken_in, axis_tag, column)]
    select_n x0 -> x1, other arithmetic: none -> 5.85 us  [tell_sources_all_here(): jnp.where(view_out == 0, before, before[::-1]).reshape(-1, *sample.shape)]
    another operation x0 -> x3, other arithmetic: none -> 5.59 us  [tell_sources_all_here(): before = jnp.stack([taken_in, arr_out])]
  transfers between devices with their start and end apart: 10 -> 11, of which waited for: 9 -> 10; matrix products, arithmetic and copies ran while one was open for 4% -> 8% of each run, Pallas kernels for 0% -> 0%
where the time goes in v1:
time: 361 us
  waiting for transfers between devices  282 us (78%)
  other arithmetic  18.7 us (5%)
  starting transfers between devices  18.1 us (5%)
  matrix products  15.7 us (4%)
  between operations  15 us (4%)
  local copies, waits for them, and re-layouts  10.5 us (3%)
    ppermute x2, waiting for transfers between devices, tell_sources_all_here(): arr_out = lax.ppermute(taken_in, axis_tag, column)  70.6 us
    all_gather x1, waiting for transfers between devices, shards(): lax.all_gather(cross_query, 'tm', axis=0, tiled=True)  61.3 us
    psum x1, waiting for transfers between devices, shards(): lax.psum(time_terms.astype(jnp.bfloat16), 'mp').astype(jnp.float32)  34.9 us
    all_to_all x1, waiting for transfers between devices, shards(): lax.all_to_all(triple, 'tm', split_axis=2, concat_axis=1, tiled=True)  30.4 us
    psum x1, waiting for transfers between devices, shards(): lax.psum(cross_terms.astype(jnp.bfloat16), 'mp').astype(jnp.float32)  28.4 us
    all_gather x1, waiting for transfers between devices, shards(): lax.all_gather(cross_merge, 'tm', axis=1, tiled=True)  26.4 us
    psum x1, waiting for transfers between devices, broadcast(): return lax.psum(block, axis)  14.1 us
    ppermute x2, starting transfers between devices, tell_sources_all_here(): arr_out = lax.ppermute(taken_in, axis_tag, column)  9.79 us
  transfers between devices with their start and end apart: 11, of which 10 were waited for; matrix products, arithmetic and copies ran while one was open for 8% of the time, Pallas kernels for 0%

profile of v1, /device:TPU:0, one launch (start us, length us, event | category | flops | bytes accessed | tf_op | source)
XLA Modules:
  0.0 360.5 jit_solution(888479125646541912)
XLA Ops:
  6.5 2.1 copy.49
  8.7 3.1 collective-permute-start
  14.1 42.9 %collective-permute-done = bf16[1,384,3,384]{3,1,2,0:T(8,128)(2,1)S(1)} collective-permute-done((bf16[1,384,3,384]{3,1,2,0:T(8,128)(2,1)S(1)}, bf16[1,384,3,384]{3,1,2,0:T(8,128)(2,1)S(1)}, u32[]{:S(2)}, u32[]{:S(2)}) %collective-permute-start) | collective-permute-done | bytes 884768 | tf_op jit(solution)/shard_map/ppermute | solution.py:23
  59.0 6.7 %collective-permute-start.1 = (bf16[2,384,3,384]{3,1,0,2:T(8,128)(2,1)}, bf16[2,384,3,384]{3,1,0,2:T(8,128)(2,1)}, u32[]{:S(2)}, u32[]{:S(2)}) collective-permute-start(bf16[2,384,3,384]{3,1,0,2:T(8,128)(2,1)} %get-tuple-element.21), channel_id=1, source_target_pairs={{0,8},{4,12},{8,0},{12,4},{1,9},{5,13},{9,1},{13,5},{2,10},{6,14},... | collective-permute-start | bytes 5308424 | tf_op jit(solution)/shard_map/ppermute | solution.py:23
  66.9 9.0 %all-gather.5.cloned.1.call-done = bf16[1536,2,384]{2,0,1:T(8,128)(2,1)} async-done(((bf16[384,2,384]{2,0,1:T(8,128)(2,1)}), bf16[1536,2,384]{2,0,1:T(8,128)(2,1)}) %all-gather.5.cloned.1.call-update) | async-done | bytes 2359312 | tf_op jit(solution)/shard_map/all_gather | solution.py:82
  77.4 61.3 %all-gather.7.cloned.1.call-done = bf16[1536,384]{1,0:T(8,128)(2,1)} async-done(((bf16[384,384]{1,0:T(8,128)(2,1)}), bf16[1536,384]{1,0:T(8,128)(2,1)}) %all-gather.7.cloned.1.call-update) | async-done | bytes 1179664 | tf_op jit(solution)/shard_map/all_gather | solution.py:81
  138.6 2.1 convolution_convert_fusion.5
  140.9 27.7 %collective-permute-done.1 = bf16[2,384,3,384]{3,1,0,2:T(8,128)(2,1)} collective-permute-done((bf16[2,384,3,384]{3,1,0,2:T(8,128)(2,1)}, bf16[2,384,3,384]{3,1,0,2:T(8,128)(2,1)}, u32[]{:S(2)}, u32[]{:S(2)}) %collective-permute-start.1) | collective-permute-done | bytes 1769504 | tf_op jit(solution)/shard_map/ppermute | solution.py:23
  168.6 3.7 %pad_maximum_fusion = bf16[2,2,384,3,384]{4,2,1,0,3:T(8,128)(2,1)} fusion(bf16[1,2,384,3,384]{4,2,1,0,3:T(8,128)(2,1)} %bitcast.28, bf16[1,2,384,3,384]{4,2,1,0,3:T(8,128)(2,1)S(1)} %get-tuple-element.20), kind=kLoop, calls=%fused_computation.5 | loop fusion | flops 1769472 | bytes 7077888 | tf_op jit(solution)/shard_map/stack | solution.py:24
  172.2 14.1 %all-reduce.4.cloned.1.call-done = bf16[1,256,2,384]{3,1,2,0:T(8,128)(2,1)} async-done(((bf16[1,256,2,384]{3,1,2,0:T(8,128)(2,1)}), bf16[1,256,2,384]{3,1,2,0:T(8,128)(2,1)}) %all-reduce.4.cloned.1.call-update) | async-done | bytes 393232 | tf_op jit(solution)/shard_map/psum | solution.py:32
  187.7 1.8 fusion.47
  191.2 26.4 %all-gather.9.cloned.1.call-done = bf16[384,1536]{1,0:T(8,128)(2,1)} async-done(((bf16[384,384]{1,0:T(8,128)(2,1)}), bf16[384,1536]{1,0:T(8,128)(2,1)}) %all-gather.9.cloned.1.call-update) | async-done | bytes 1179664 | tf_op jit(solution)/shard_map/all_gather | solution.py:83
  217.6 2.7 convolution_convert_fusion.2
  220.4 5.8 %reverse_select_fusion = bf16[2,2,384,3,384]{4,2,1,0,3:T(8,128)(2,1)} fusion(bf16[2,2,384,3,384]{4,2,1,0,3:T(8,128)(2,1)} %pad_maximum_fusion, pred[]{:T(512)S(6)} %eq.49), kind=kLoop, calls=%fused_computation.4 | loop fusion | flops 1769472 | bytes 7077889 | tf_op jit(solution)/shard_map/jit(_where)/select_n | solution.py:26
  226.3 28.4 %all-reduce.6.cloned.1.call-done = bf16[256,1536]{1,0:T(8,128)(2,1)} async-done(((bf16[256,1536]{1,0:T(8,128)(2,1)}), bf16[256,1536]{1,0:T(8,128)(2,1)}) %all-reduce.6.cloned.1.call-update) | async-done | bytes 786448 | tf_op jit(solution)/shard_map/psum | solution.py:122
  256.7 3.3 fusion.14
  261.3 4.6 %all-to-all-start = ((bf16[1,1,256,3,384]{4,3,1,0,2:T(4,128)(2,1)}), bf16[1,1,256,3,384]{4,3,1,0,2:T(4,128)(2,1)}, u32[]{:S(2)}, u32[]{:S(2)}) async-start(bf16[1,1,256,3,384]{4,3,1,0,2:T(4,128)(2,1)} %copy.55), calls=%async_computation | async-start | bytes 1572864 | tf_op jit(solution)/shard_map/all_to_all | solution.py:134
  266.6 30.4 %all-to-all-done = bf16[1,1,256,3,384]{4,3,1,0,2:T(4,128)(2,1)} async-done(((bf16[1,1,256,3,384]{4,3,1,0,2:T(4,128)(2,1)}), bf16[1,1,256,3,384]{4,3,1,0,2:T(4,128)(2,1)}, u32[]{:S(2)}, u32[]{:S(2)}) %all-to-all-start) | async-done | bytes 589856 | tf_op jit(solution)/shard_map/all_to_all | solution.py:134
  296.9 2.7 reshape.231
  303.8 3.6 all-to-all-start.1
  307.4 6.2 %all-to-all-done.1 = bf16[1,4,64,384]{3,2,0,1:T(8,128)(2,1)S(1)} async-done(((bf16[1,4,64,384]{3,2,0,1:T(8,128)(2,1)}), bf16[1,4,64,384]{3,2,0,1:T(8,128)(2,1)S(1)}, u32[]{:S(2)}, u32[]{:S(2)}) %all-to-all-start.1) | async-done | bytes 196640 | tf_op jit(solution)/shard_map/all_to_all | solution.py:158
  313.6 2.7 convolution_convert_fusion.1
  316.4 34.9 %all-reduce.8.cloned.1.call-done = bf16[256,1536]{1,0:T(8,128)(2,1)} async-done(((bf16[256,1536]{1,0:T(8,128)(2,1)}), bf16[256,1536]{1,0:T(8,128)(2,1)}) %all-reduce.8.cloned.1.call-update) | async-done | bytes 786448 | tf_op jit(solution)/shard_map/psum | solution.py:164
  351.3 2.4 fusion.10
  (60 shorter events, 17.1 us)
Async XLA Ops:
  6.5 6.0 %copy-start = (f32[8,6,1536]{2,0,1:T(8,128)S(1)}, f32[8,6,1536]{2,0,1:T(8,128)}, u32[]{:S(2)}) copy-start(f32[8,6,1536]{2,0,1:T(8,128)} %param.13) | copy-start | bytes 884740
  6.5 2.2 copy-start.3
  6.5 6.3 %copy-start.1 = (bf16[1,1,256,1536]{3,2,1,0:T(8,128)(2,1)S(1)}, bf16[1,1,256,1536]{3,2,1,0:T(8,128)(2,1)}, u32[]{:S(2)}) copy-start(bf16[1,1,256,1536]{3,2,1,0:T(8,128)(2,1)} %param.12) | copy-start | bytes 2359300
  6.5 69.3 %all-gather.5.cloned.1.call-start = ((), (), s32[]{:S(2)}) async-start(), calls=%async_computation.2 | async-start | bytes 2949120 | tf_op jit(solution)/shard_map/all_gather | solution.py:82
  8.7 130.0 %all-gather.7.cloned.1.call-start = ((), (), s32[]{:S(2)}) async-start(), calls=%async_computation.4 | async-start | bytes 1474560 | tf_op jit(solution)/shard_map/all_gather | solution.py:81
  8.7 48.3 %collective-permute-start = (bf16[1,384,3,384]{3,1,2,0:T(8,128)(2,1)S(1)}, bf16[1,384,3,384]{3,1,2,0:T(8,128)(2,1)S(1)}, u32[]{:S(2)}, u32[]{:S(2)}) collective-permute-start(bf16[1,384,3,384]{3,1,2,0:T(8,128)(2,1)S(1)} %bitcast.105), channel_id=1, source_target_pairs={{0,4},{4,0},{8,12},{12,8},{1,5},{5,1},{9,13},{13,9},{2,6},{6,2},{1... | collective-permute-start | bytes 2654216 | tf_op jit(solution)/shard_map/ppermute | solution.py:23
  11.8 174.5 %all-reduce.4.cloned.1.call-start = ((), (), s32[]{:S(2)}) async-start(), calls=%async_computation.3 | async-start | bytes 786432 | tf_op jit(solution)/shard_map/psum | solution.py:32
  59.0 109.6 %collective-permute-start.1 = (bf16[2,384,3,384]{3,1,0,2:T(8,128)(2,1)}, bf16[2,384,3,384]{3,1,0,2:T(8,128)(2,1)}, u32[]{:S(2)}, u32[]{:S(2)}) collective-permute-start(bf16[2,384,3,384]{3,1,0,2:T(8,128)(2,1)} %get-tuple-element.21), channel_id=1, source_target_pairs={{0,8},{4,12},{8,0},{12,4},{1,9},{5,13},{9,1},{13,5},{2,10},{6,14},... | collective-permute-start | bytes 5308424 | tf_op jit(solution)/shard_map/ppermute | solution.py:23
  76.7 140.9 %all-gather.9.cloned.1.call-start = ((), (), s32[]{:S(2)}) async-start(), calls=%async_computation.5 | async-start | bytes 1474560 | tf_op jit(solution)/shard_map/all_gather | solution.py:83
  77.3 177.3 %all-reduce.6.cloned.1.call-start = ((), (), s32[]{:S(2)}) async-start(), calls=%async_computation.6 | async-start | bytes 1572864 | tf_op jit(solution)/shard_map/psum | solution.py:122
  254.6 1.6 copy-start.2
  259.9 6.6 %copy-start.5 = (s32[1,4,256]{2,1,0:T(4,128)S(1)}, s32[1,4,256]{2,1,0:T(4,128)}, u32[]{:S(2)}) copy-start(s32[1,4,256]{2,1,0:T(4,128)} %param.16) | copy-start | bytes 12292
  261.3 35.6 %all-to-all-start = ((bf16[1,1,256,3,384]{4,3,1,0,2:T(4,128)(2,1)}), bf16[1,1,256,3,384]{4,3,1,0,2:T(4,128)(2,1)}, u32[]{:S(2)}, u32[]{:S(2)}) async-start(bf16[1,1,256,3,384]{4,3,1,0,2:T(4,128)(2,1)} %copy.55), calls=%async_computation | async-start | bytes 1572864 | tf_op jit(solution)/shard_map/all_to_all | solution.py:134
  265.9 41.5 %all-gather.11.cloned.1.call-start = ((), (), s32[]{:S(2)}) async-start(), calls=%async_computation.7 | async-start | bytes 1474560 | tf_op jit(solution)/shard_map/all_gather | solution.py:85
  300.7 1.4 copy-start.4
  303.8 9.8 %all-to-all-start.1 = ((bf16[1,4,64,384]{3,2,0,1:T(8,128)(2,1)}), bf16[1,4,64,384]{3,2,0,1:T(8,128)(2,1)S(1)}, u32[]{:S(2)}, u32[]{:S(2)}) async-start(bf16[1,4,64,384]{3,2,0,1:T(8,128)(2,1)} %bitcast.38), calls=%async_computation.1 | async-start | bytes 393216 | tf_op jit(solution)/shard_map/all_to_all | solution.py:158
  307.4 43.9 %all-reduce.8.cloned.1.call-start = ((), (), s32[]{:S(2)}) async-start(), calls=%async_computation.8 | async-start | bytes 1572864 | tf_op jit(solution)/shard_map/psum | solution.py:164
Sparse Core Ops, SparseCore 0:
  8.9 66.8 all-gather.4
  77.4 61.1 all-gather.6
  141.0 45.2 all-reduce.3
  187.9 29.7 all-gather.8
  220.5 34.0 all-reduce.5
  268.1 36.4 all-gather.10
  316.5 34.7 all-reduce.7
